TPU v7x, 256 devices: a whole 4x4x8 slice. The times are simulated.
256 devices in a mesh: row: 64 (over z, x, core), col: 4 (over y).
Axes of the slice: x: 4, y: 4, z: 8, core: 2. Of those that a mesh axis runs over, the one named last changes fastest.
Arguments:
- eigen_vectors: float32 [65536, 2048], P('row', 'col'), may hold values from -6 to 6
- panel_first: float32 [65536, 512], P('row', 'col'), may hold values from -0.0234375 to 0.0234375
- panel_second: float32 [65536, 512], P('row', 'col'), may hold values from -0.0234375 to 0.0234375
- factor_first: float32 [512, 512], replicated, as said below
- factor_second: float32 [512, 512], replicated, as said below
Outputs:
- transformed: float32 [65536, 2048], P('row', 'col')
Inputs may be any that keep to these rules, and one draw needn't show every extreme that they name: factor_first is upper triangular. factor_second is upper triangular.
All inputs are finite; a program needn't handle non-finite values.
Results may differ from a plain program's by a relative error of at most 0.0001.
Values sent between devices are 32-bit elements; how exact they have to be, the bound alone decides.
A program may use at most 64 MiB of HBM per device.

v0:
```python
import jax
import jax.numpy as jnp
from jax import lax
from jax.sharding import PartitionSpec as P


def local_dot(left, right):
    return jnp.dot(left, right, precision=lax.Precision.HIGHEST, preferred_element_type=jnp.float32)


def on_device(eigen_vectors, panel_first, panel_second, factor_first, factor_second):
    vectors_first, vectors_second = (
        lax.all_gather(panel_first, "col", axis=1, tiled=True),
        lax.all_gather(panel_second, "col", axis=1, tiled=True),
    )
    updated = eigen_vectors
    for vectors, factor in ((vectors_second, factor_second), (vectors_first, factor_first)):
        projected = lax.psum(local_dot(vectors.T, updated), "row")
        updated = updated - local_dot(vectors, local_dot(factor, projected))
    return updated


def solution(mesh):
    return jax.shard_map(
        on_device,
        mesh=mesh,
        in_specs=(P("row", "col"), P("row", "col"), P("row", "col"), P(), P()),
        out_specs=P("row", "col"),
        check_vma=False,
    )
```

profile of v0, /device:TPU:2, one launch (start us, length us, event | category | flops | bytes accessed | tf_op | source)
XLA Modules:
  0.0 489.9 jit_solution(13519576373823585658)
XLA Ops:
  6.5 0.0 copy-start
  6.5 0.0 all-gather.3.cloned.1.call-start
  6.5 0.7 all-gather.3.cloned.1.call-update
  7.3 0.0 all-reduce.3.cloned.1.call-start
  7.3 41.9 %all-gather.3.cloned.1.call-done = f32[1024,512]{1,0:T(8,128)} async-done(((f32[1024,128]{1,0:T(8,128)}), f32[1024,512]{1,0:T(8,128)}) %all-gather.3.cloned.1.call-update) | async-done | bytes 2097168 | tf_op jit(solution)/shard_map/all_gather | solution.py:14
  49.2 0.0 copy-start.3
  49.2 6.9 %fusion = f32[512,512]{1,0:T(8,128)} fusion(f32[1024,512]{1,0:T(8,128)} %all-gather.3.cloned.1.call-done, f32[1024,512]{1,0:T(8,128)} %param.5), kind=kOutput, calls=%fused_computation.3 | convolution fusion | flops 3221225472 | bytes 5242880 | tf_op jit(solution)/shard_map/dot_general | solution.py:8
  56.1 0.0 all-reduce.3.cloned.1.call-update
  56.1 0.0 all-gather.5.cloned.1.call-start
  56.1 0.7 all-gather.5.cloned.1.call-update
  56.8 0.0 all-reduce.5.cloned.1.call-start
  56.9 0.0 copy-done.3
  56.9 1.8 copy.6
  58.7 183.9 %all-reduce.3.cloned.1.call-done = f32[512,512]{1,0:T(8,128)} async-done(((f32[512,512]{1,0:T(8,128)}), f32[512,512]{1,0:T(8,128)}) %all-reduce.3.cloned.1.call-update) | async-done | bytes 1048592 | tf_op jit(solution)/shard_map/psum | solution.py:18
  242.6 0.0 copy-done
  242.6 0.0 copy-start.1
  242.6 4.8 fusion.1
  247.4 0.0 copy-done.1
  247.5 5.2 %bitcast_subtract_fusion.1 = f32[1024,512]{0,1:T(8,128)S(1)} fusion(f32[1024,512]{0,1:T(8,128)} %copy.6, f32[512,512]{1,0:T(8,128)S(1)} %fusion.1, f32[1024,512]{1,0:T(8,128)S(1)} %copy-done.1), kind=kOutput, calls=%fused_computation.1 | convolution fusion | flops 3221749760 | bytes 7340032 | tf_op jit(solution)/shard_map/dot_general | solution.py:8
  252.6 26.6 %all-gather.5.cloned.1.call-done = f32[1024,512]{1,0:T(8,128)} async-done(((f32[1024,128]{1,0:T(8,128)}), f32[1024,512]{1,0:T(8,128)}) %all-gather.5.cloned.1.call-update) | async-done | bytes 2097168 | tf_op jit(solution)/shard_map/all_gather | solution.py:13
  279.2 6.1 %convolution_bitcast_fusion = f32[512,512]{0,1:T(8,128)} fusion(f32[1024,512]{0,1:T(8,128)S(1)} %bitcast_subtract_fusion.1, f32[1024,512]{1,0:T(8,128)} %all-gather.5.cloned.1.call-done), kind=kOutput, calls=%fused_computation.2 | convolution fusion | flops 3221225472 | bytes 5242880 | tf_op jit(solution)/shard_map/dot_general | solution.py:8
  285.3 0.0 all-reduce.5.cloned.1.call-update
  285.3 186.5 %all-reduce.5.cloned.1.call-done = f32[512,512]{0,1:T(8,128)} async-done(((f32[512,512]{0,1:T(8,128)}), f32[512,512]{0,1:T(8,128)}) %all-reduce.5.cloned.1.call-update) | async-done | bytes 1048592 | tf_op jit(solution)/shard_map/psum | solution.py:18
  471.8 0.0 copy-start.2
  471.8 3.5 fusion.2
  475.4 0.0 copy-done.2
  475.4 5.1 %bitcast_subtract_fusion = f32[1024,512]{0,1:T(8,128)} fusion(f32[1024,512]{0,1:T(8,128)S(1)} %bitcast_subtract_fusion.1, f32[512,512]{1,0:T(8,128)S(1)} %fusion.2, f32[1024,512]{1,0:T(8,128)S(1)} %copy-done.2), kind=kOutput, calls=%fused_computation | convolution fusion | flops 3221749760 | bytes 7340032 | tf_op jit(solution)/shard_map/dot_general | solution.py:8
  480.5 2.9 copy.7
Async XLA Ops:
  6.5 236.1 %copy-start = (f32[512,512]{1,0:T(8,128)S(1)}, f32[512,512]{1,0:T(8,128)}, u32[]{:S(2)}) copy-start(f32[512,512]{1,0:T(8,128)} %param.9) | copy-start | bytes 3145732
  6.5 42.7 %all-gather.3.cloned.1.call-start = ((), (), s32[]{:S(2)}) async-start(), calls=%async_computation | async-start | bytes 2621440 | tf_op jit(solution)/shard_map/all_gather | solution.py:14
  7.3 235.3 %all-reduce.3.cloned.1.call-start = ((), (), s32[]{:S(2)}) async-start(), calls=%async_computation.1 | async-start | bytes 2097152 | tf_op jit(solution)/shard_map/psum | solution.py:18
  49.2 7.7 %copy-start.3 = (f32[1024,512]{1,0:T(8,128)S(1)}, f32[1024,512]{1,0:T(8,128)}, u32[]{:S(2)}) copy-start(f32[1024,512]{1,0:T(8,128)} %param.5) | copy-start | bytes 6291460
  56.1 223.1 %all-gather.5.cloned.1.call-start = ((), (), s32[]{:S(2)}) async-start(), calls=%async_computation.2 | async-start | bytes 2621440 | tf_op jit(solution)/shard_map/all_gather | solution.py:13
  56.8 415.0 %all-reduce.5.cloned.1.call-start = ((), (), s32[]{:S(2)}) async-start(), calls=%async_computation.3 | async-start | bytes 2097152 | tf_op jit(solution)/shard_map/psum | solution.py:18
  242.6 4.9 copy-start.1
  471.8 3.6 copy-start.2
Sparse Core Ops, SparseCore 0:
  9.2 40.0 all-gather.2
  56.2 186.3 all-reduce.2
  244.5 34.6 all-gather.4
  285.4 186.3 all-reduce.4
where the time goes:
time: 490 us
  waiting for transfers between devices  440 us (90%)
  matrix products  31.6 us (6%)
  between operations  13.2 us (3%)
    psum x2, waiting for transfers between devices, on_device(): projected = lax.psum(local_dot(vectors.T, updated), 'row')  370 us
    all_gather x1, waiting for transfers between devices, on_device(): lax.all_gather(panel_second, 'col', axis=1, tiled=True)  41.9 us
    dot_general x6, matrix products, local_dot(): jnp.dot(left, right, precision=lax.Precision.HIGHEST, preferred_element_t...  31.6 us
    all_gather x1, waiting for transfers between devices, on_device(): lax.all_gather(panel_first, 'col', axis=1, tiled=True)  26.6 us
  transfers between devices with their start and end apart: 4, of which 4 were waited for; matrix products, arithmetic and copies ran while one was open for 2% of the time, Pallas kernels for 0%

commit v1 on v0

--- a/solution.py
+++ b/solution.py
@@ -10,7 +10,9 @@
 
 def on_device(eigen_vectors, panel_first, panel_second, factor_first, factor_second):
     vectors_first, vectors_second = (
-        lax.all_gather(panel_first, "col", axis=1, tiled=True),
+        jnp.concatenate(
+            lax.all_to_all(jnp.stack([panel_first] * lax.axis_size("col")), "col", 0, 0), axis=1
+        ),
         lax.all_gather(panel_second, "col", axis=1, tiled=True),
     )
     updated = eigen_vectors

time: 490 us -> 474 us (0.967)
  waiting for transfers between devices: 440 us -> 416 us
    all_gather x1 -> x0, waiting for transfers between devices: 26.6 us -> none  [on_device(): lax.all_gather(panel_first, 'col', axis=1, tiled=True)]
    all_gather x1, waiting for transfers between devices: 41.9 us -> 47.2 us  [on_device(): lax.all_gather(panel_second, 'col', axis=1, tiled=True)]
  transfers between devices with their start and end apart: 4 -> 4, of which waited for: 4 -> 3; matrix products, arithmetic and copies ran while one was open for 2% -> 4% of each run, Pallas kernels for 0% -> 0%
where the time goes in v1:
time: 474 us; the launch traced here: 473 us
  waiting for transfers between devices  416 us (88%)
  matrix products  32.3 us (7%)
  between operations  13.2 us (3%)
  local copies, waits for them, and re-layouts  7.54 us (2%)
    psum x2, waiting for transfers between devices, on_device(): projected = lax.psum(local_dot(vectors.T, updated), 'row')  368 us
    all_gather x1, waiting for transfers between devices, on_device(): lax.all_gather(panel_second, 'col', axis=1, tiled=True)  47.2 us
    dot_general x6, matrix products, local_dot(): jnp.dot(left, right, precision=lax.Precision.HIGHEST, preferred_element_t...  32.3 us
  transfers between devices with their start and end apart: 4, of which 3 were waited for; matrix products, arithmetic and copies ran while one was open for 4% of the time, Pallas kernels for 0%

profile of v1, /device:TPU:2, one launch (start us, length us, event | category | flops | bytes accessed | tf_op | source)
XLA Modules:
  0.0 473.4 jit_solution(1854935202438279240)
XLA Ops:
  6.5 0.0 copy-start
  6.5 0.0 all-gather.2.cloned.1.call-start
  6.5 0.7 all-gather.2.cloned.1.call-update
  7.3 1.2 copy.9
  8.5 1.6 stack.2
  10.1 0.0 copy-start.2
  10.1 4.6 all-to-all-start
  14.7 0.0 all-reduce.3.cloned.1.call-start
  14.7 47.2 %all-gather.2.cloned.1.call-done = f32[1024,512]{1,0:T(8,128)} async-done(((f32[1024,128]{1,0:T(8,128)}), f32[1024,512]{1,0:T(8,128)}) %all-gather.2.cloned.1.call-update) | async-done | bytes 2097168 | tf_op jit(solution)/shard_map/all_gather | solution.py:16
  61.9 0.0 copy-done.2
  61.9 6.1 %fusion = f32[512,512]{1,0:T(8,128)} fusion(f32[1024,512]{1,0:T(8,128)} %all-gather.2.cloned.1.call-done, f32[1024,512]{1,0:T(8,128)S(1)} %copy-done.2), kind=kOutput, calls=%fused_computation.3 | convolution fusion | flops 3221225472 | bytes 5242880 | tf_op jit(solution)/shard_map/dot_general | solution.py:8
  68.0 0.0 all-reduce.3.cloned.1.call-update
  68.0 0.0 all-reduce.5.cloned.1.call-start
  68.1 1.8 copy.8
  69.9 184.7 %all-reduce.3.cloned.1.call-done = f32[512,512]{1,0:T(8,128)} async-done(((f32[512,512]{1,0:T(8,128)}), f32[512,512]{1,0:T(8,128)}) %all-reduce.3.cloned.1.call-update) | async-done | bytes 1048592 | tf_op jit(solution)/shard_map/psum | solution.py:20
  254.6 0.0 copy-done
  254.6 0.0 copy-start.1
  254.6 4.8 %fusion.1 = f32[512,512]{1,0:T(8,128)S(1)} fusion(f32[512,512]{1,0:T(8,128)} %all-reduce.3.cloned.1.call-done, f32[512,512]{1,0:T(8,128)S(1)} %copy-done), kind=kOutput, calls=%fused_computation.4 | convolution fusion | flops 1610612736 | bytes 3145728 | tf_op jit(solution)/shard_map/dot_general | solution.py:8
  259.5 0.0 copy-done.1
  259.5 5.2 %bitcast_subtract_fusion.1 = f32[1024,512]{0,1:T(8,128)S(1)} fusion(f32[1024,512]{0,1:T(8,128)} %copy.8, f32[512,512]{1,0:T(8,128)S(1)} %fusion.1, f32[1024,512]{1,0:T(8,128)S(1)} %copy-done.1), kind=kOutput, calls=%fused_computation.1 | convolution fusion | flops 3221749760 | bytes 7340032 | tf_op jit(solution)/shard_map/dot_general | solution.py:8
  264.7 0.0 all-to-all-done
  264.7 6.1 %convolution_bitcast_fusion = f32[512,512]{0,1:T(8,128)} fusion(f32[1024,512]{0,1:T(8,128)S(1)} %bitcast_subtract_fusion.1, f32[1024,512]{0,1:T(8,128)} %bitcast.2), kind=kOutput, calls=%fused_computation.2 | convolution fusion | flops 3221225472 | bytes 5242880 | tf_op jit(solution)/shard_map/dot_general | solution.py:8
  270.7 0.0 all-reduce.5.cloned.1.call-update
  270.8 183.1 %all-reduce.5.cloned.1.call-done = f32[512,512]{0,1:T(8,128)} async-done(((f32[512,512]{0,1:T(8,128)}), f32[512,512]{0,1:T(8,128)}) %all-reduce.5.cloned.1.call-update) | async-done | bytes 1048592 | tf_op jit(solution)/shard_map/psum | solution.py:20
  453.9 3.6 fusion.2
  457.5 6.5 %bitcast_subtract_fusion = f32[1024,512]{0,1:T(8,128)} fusion(f32[1024,512]{0,1:T(8,128)S(1)} %bitcast_subtract_fusion.1, f32[512,512]{1,0:T(8,128)S(1)} %fusion.2, f32[1024,512]{0,1:T(8,128)} %bitcast.2), kind=kOutput, calls=%fused_computation | convolution fusion | flops 3221749760 | bytes 7340032 | tf_op jit(solution)/shard_map/dot_general | solution.py:8
  464.0 2.9 copy.10
Async XLA Ops:
  6.5 248.1 %copy-start = (f32[512,512]{1,0:T(8,128)S(1)}, f32[512,512]{1,0:T(8,128)}, u32[]{:S(2)}) copy-start(f32[512,512]{1,0:T(8,128)} %param.9) | copy-start | bytes 3145732
  6.5 55.4 %all-gather.2.cloned.1.call-start = ((), (), s32[]{:S(2)}) async-start(), calls=%async_computation.1 | async-start | bytes 2621440 | tf_op jit(solution)/shard_map/all_gather | solution.py:16
  10.1 51.8 %copy-start.2 = (f32[1024,512]{1,0:T(8,128)S(1)}, f32[1024,512]{1,0:T(8,128)}, u32[]{:S(2)}) copy-start(f32[1024,512]{1,0:T(8,128)} %param.5) | copy-start | bytes 6291460
  10.1 254.5 %all-to-all-start = ((f32[4,1024,128]{1,2,0:T(8,128)}), f32[4,1024,128]{1,2,0:T(8,128)}, u32[]{:S(2)}, u32[]{:S(2)}) async-start(f32[4,1024,128]{1,2,0:T(8,128)} %stack.2), calls=%async_computation | async-start | bytes 4194304 | tf_op jit(solution)/shard_map/all_to_all | solution.py:14
  14.7 239.9 %all-reduce.3.cloned.1.call-start = ((), (), s32[]{:S(2)}) async-start(), calls=%async_computation.2 | async-start | bytes 2097152 | tf_op jit(solution)/shard_map/psum | solution.py:20
  68.0 385.8 %all-reduce.5.cloned.1.call-start = ((), (), s32[]{:S(2)}) async-start(), calls=%async_computation.3 | async-start | bytes 2097152 | tf_op jit(solution)/shard_map/psum | solution.py:20
  254.6 4.9 %copy-start.1 = (f32[1024,512]{1,0:T(8,128)S(1)}, f32[1024,512]{1,0:T(8,128)}, u32[]{:S(2)}) copy-start(f32[1024,512]{1,0:T(8,128)} %all-gather.2.cloned.1.call-done) | copy-start | bytes 6291460
Sparse Core Ops, SparseCore 0:
  9.2 52.7 all-gather.1
  68.2 186.3 all-reduce.2
  270.9 182.9 all-reduce.4

commit v2 on v0

--- a/solution.py
+++ b/solution.py
@@ -2,6 +2,27 @@
 import jax.numpy as jnp
 from jax import lax
 from jax.sharding import PartitionSpec as P
+
+
+def ring_gather(value, axis, dim):
+    length, position, span = (lax.axis_size(axis), lax.axis_index(axis), value.shape[dim])
+    ahead = [(i, (i + 1) % length) for i in range(length)]
+    left = [(i, (i - 1) % length) for i in range(length)]
+    filled = jnp.zeros((*value.shape[:dim], length * span, *value.shape[dim + 1 :]), value.dtype)
+    filled = lax.dynamic_update_slice_in_dim(filled, value, position * span, axis=dim)
+    from_left = from_right = value
+    middle = length // 2
+    for hop in range(1, middle + 1):
+        from_left = lax.ppermute(from_left, axis, ahead)
+        filled = lax.dynamic_update_slice_in_dim(
+            filled, from_left, (position - hop) % length * span, axis=dim
+        )
+        if hop < length - middle:
+            from_right = lax.ppermute(from_right, axis, left)
+            filled = lax.dynamic_update_slice_in_dim(
+                filled, from_right, (position + hop) % length * span, axis=dim
+            )
+    return filled
 
 
 def local_dot(left, right):
@@ -11,7 +32,7 @@
 def on_device(eigen_vectors, panel_first, panel_second, factor_first, factor_second):
     vectors_first, vectors_second = (
         lax.all_gather(panel_first, "col", axis=1, tiled=True),
-        lax.all_gather(panel_second, "col", axis=1, tiled=True),
+        ring_gather(panel_second, "col", 1),
     )
     updated = eigen_vectors
     for vectors, factor in ((vectors_second, factor_second), (vectors_first, factor_first)):

time: 490 us -> 445 us (0.908)
  waiting for transfers between devices: 440 us -> 395 us
    all_gather x1 -> x0, waiting for transfers between devices: 41.9 us -> none  [on_device(): lax.all_gather(panel_second, 'col', axis=1, tiled=True)]
    all_gather x1, waiting for transfers between devices: 26.6 us -> 0.03 us  [on_device(): lax.all_gather(panel_first, 'col', axis=1, tiled=True)]
    ppermute x0 -> x3, waiting for transfers between devices: none -> 25.3 us  [the longest x2 25.2 us: ring_gather(): from_left = lax.ppermute(from_left, axis, ahead)]
  transfers between devices with their start and end apart: 4 -> 6, of which waited for: 4 -> 4; matrix products, arithmetic and copies ran while one was open for 2% -> 2% of each run, Pallas kernels for 0% -> 0%
where the time goes in v2:
time: 445 us
  waiting for transfers between devices  395 us (89%)
  matrix products  29.7 us (7%)
  between operations  15 us (3%)
    psum x2, waiting for transfers between devices, on_device(): projected = lax.psum(local_dot(vectors.T, updated), 'row')  369 us
    dot_general x6, matrix products, local_dot(): jnp.dot(left, right, precision=lax.Precision.HIGHEST, preferred_element_t...  29.7 us
    ppermute x2, waiting for transfers between devices, ring_gather(): from_left = lax.ppermute(from_left, axis, ahead)  25.2 us
  transfers between devices with their start and end apart: 6, of which 4 were waited for; matrix products, arithmetic and copies ran while one was open for 2% of the time, Pallas kernels for 0%

profile of v2, /device:TPU:2, one launch (start us, length us, event | category | flops | bytes accessed | tf_op | source)
XLA Modules:
  0.0 445.1 jit_solution(15920913346903934602)
XLA Ops:
  7.4 0.0 copy-start
  7.4 0.0 copy-start.4
  7.4 0.0 all-reduce.3.cloned.1.call-start
  7.4 1.6 collective-permute-start
  9.0 1.7 collective-permute-start.1
  10.6 11.9 %collective-permute-done = f32[1024,128]{1,0:T(8,128)S(1)} collective-permute-done((f32[1024,128]{1,0:T(8,128)}, f32[1024,128]{1,0:T(8,128)S(1)}, u32[]{:S(2)}, u32[]{:S(2)}) %collective-permute-start) | collective-permute-done | bytes 524320 | tf_op jit(solution)/shard_map/ppermute | solution.py:16
  22.6 0.3 collective-permute-start.2
  22.8 0.2 broadcast_in_dim.3
  23.1 0.0 copy-done.4
  23.1 0.0 copy-start.2
  23.1 0.1 constant_dynamic-update-slice_fusion.3
  23.2 0.1 constant_dynamic-update-slice_fusion.2
  23.3 0.0 collective-permute-done.1
  23.3 0.1 constant_dynamic-update-slice_fusion.1
  23.3 13.3 %collective-permute-done.2 = f32[1024,128]{1,0:T(8,128)S(1)} collective-permute-done((f32[1024,128]{1,0:T(8,128)S(1)}, f32[1024,128]{1,0:T(8,128)S(1)}, u32[]{:S(2)}, u32[]{:S(2)}) %collective-permute-start.2) | collective-permute-done | bytes 524320 | tf_op jit(solution)/shard_map/ppermute | solution.py:16
  36.7 0.1 constant_dynamic-update-slice_fusion
  36.7 0.0 copy-start.1
  36.7 1.3 copy-done.1
  38.0 0.0 copy-done.2
  38.1 4.6 %fusion = f32[512,512]{1,0:T(8,128)} fusion(f32[1024,512]{1,0:T(8,128)S(1)} %constant_dynamic-update-slice_fusion, f32[1024,512]{1,0:T(8,128)S(1)} %copy-done.2), kind=kOutput, calls=%fused_computation.7 | convolution fusion | flops 3221225472 | bytes 5242880 | tf_op jit(solution)/shard_map/dot_general | solution.py:29
  42.7 0.0 all-reduce.3.cloned.1.call-update
  42.7 0.0 all-gather.2.cloned.1.call-start
  42.7 0.5 all-gather.2.cloned.1.call-update
  43.3 0.2 all-reduce.5.cloned.1.call-start
  43.5 186.0 %all-reduce.3.cloned.1.call-done = f32[512,512]{1,0:T(8,128)} async-done(((f32[512,512]{1,0:T(8,128)}), f32[512,512]{1,0:T(8,128)}) %all-reduce.3.cloned.1.call-update) | async-done | bytes 1048592 | tf_op jit(solution)/shard_map/psum | solution.py:39
  229.4 0.0 copy-done
  229.5 4.7 %fusion.1 = f32[512,512]{1,0:T(8,128)S(1)} fusion(f32[512,512]{1,0:T(8,128)} %all-reduce.3.cloned.1.call-done, f32[512,512]{1,0:T(8,128)S(1)} %copy-done), kind=kOutput, calls=%fused_computation.8 | convolution fusion | flops 1610612736 | bytes 3145728 | tf_op jit(solution)/shard_map/dot_general | solution.py:29
  234.2 5.7 %convolution_subtract_fusion = f32[1024,512]{1,0:T(8,128)S(1)} fusion(f32[1024,512]{1,0:T(8,128)} %param.5, f32[1024,512]{1,0:T(8,128)} %copy-done.1, f32[512,512]{1,0:T(8,128)S(1)} %fusion.1), kind=kOutput, calls=%fused_computation.1 | convolution fusion | flops 3221749760 | bytes 7340032 | tf_op jit(solution)/shard_map/dot_general | solution.py:29
  239.9 0.0 all-gather.2.cloned.1.call-done
  239.9 6.1 %convolution_bitcast_fusion = f32[512,512]{0,1:T(8,128)} fusion(f32[1024,512]{1,0:T(8,128)S(1)} %convolution_subtract_fusion, f32[1024,512]{1,0:T(8,128)} %all-gather.2.cloned.1.call-done), kind=kOutput, calls=%fused_computation.2 | convolution fusion | flops 3221225472 | bytes 5242880 | tf_op jit(solution)/shard_map/dot_general | solution.py:29
  245.9 0.0 all-reduce.5.cloned.1.call-update
  246.0 183.1 %all-reduce.5.cloned.1.call-done = f32[512,512]{0,1:T(8,128)} async-done(((f32[512,512]{0,1:T(8,128)}), f32[512,512]{0,1:T(8,128)}) %all-reduce.5.cloned.1.call-update) | async-done | bytes 1048592 | tf_op jit(solution)/shard_map/psum | solution.py:39
  429.0 0.0 copy-start.3
  429.0 3.8 fusion.2
  432.8 0.0 copy-done.3
  432.8 4.8 %bitcast_subtract_fusion = f32[1024,512]{1,0:T(8,128)} fusion(f32[1024,512]{1,0:T(8,128)S(1)} %convolution_subtract_fusion, f32[512,512]{1,0:T(8,128)S(1)} %fusion.2, f32[1024,512]{1,0:T(8,128)S(1)} %copy-done.3), kind=kOutput, calls=%fused_computation | convolution fusion | flops 3221749760 | bytes 7340032 | tf_op jit(solution)/shard_map/dot_general | solution.py:29
Async XLA Ops:
  7.4 222.1 %copy-start = (f32[512,512]{1,0:T(8,128)S(1)}, f32[512,512]{1,0:T(8,128)}, u32[]{:S(2)}) copy-start(f32[512,512]{1,0:T(8,128)} %param.9) | copy-start | bytes 3145732
  7.4 15.7 %copy-start.4 = (f32[1024,128]{1,0:T(8,128)S(1)}, f32[1024,128]{1,0:T(8,128)}, u32[]{:S(2)}) copy-start(f32[1024,128]{1,0:T(8,128)} %param.7) | copy-start | bytes 1572868
  7.4 222.1 %all-reduce.3.cloned.1.call-start = ((), (), s32[]{:S(2)}) async-start(), calls=%async_computation | async-start | bytes 2097152 | tf_op jit(solution)/shard_map/psum | solution.py:39
  7.4 15.2 %collective-permute-start = (f32[1024,128]{1,0:T(8,128)}, f32[1024,128]{1,0:T(8,128)S(1)}, u32[]{:S(2)}, u32[]{:S(2)}) collective-permute-start(f32[1024,128]{1,0:T(8,128)} %param.7), channel_id=1, source_target_pairs={{0,1},{1,2},{2,3},{3,0},{4,5},{5,6},{6,7},{7,4},{8,9},{9,10},{10,1... | collective-permute-start | bytes 1572872 | tf_op jit(solution)/shard_map/ppermute | solution.py:16
  9.0 14.3 %collective-permute-start.1 = (f32[1024,128]{1,0:T(8,128)}, f32[1024,128]{1,0:T(8,128)S(1)}, u32[]{:S(2)}, u32[]{:S(2)}) collective-permute-start(f32[1024,128]{1,0:T(8,128)} %param.7), channel_id=1, source_target_pairs={{0,3},{1,0},{2,1},{3,2},{4,7},{5,4},{6,5},{7,6},{8,11},{9,8},{10,9... | collective-permute-start | bytes 1572872 | tf_op jit(solution)/shard_map/ppermute | solution.py:21
  22.6 14.1 %collective-permute-start.2 = (f32[1024,128]{1,0:T(8,128)S(1)}, f32[1024,128]{1,0:T(8,128)S(1)}, u32[]{:S(2)}, u32[]{:S(2)}) collective-permute-start(f32[1024,128]{1,0:T(8,128)S(1)} %collective-permute-done), channel_id=1, source_target_pairs={{0,1},{1,2},{2,3},{3,0},{4,5},{5,6},{6,7},{7,4},{8,9},{9,10},{10,1... | collective-permute-start | bytes 1572872 | tf_op jit(solution)/shard_map/ppermute | solution.py:16
  23.1 15.0 %copy-start.2 = (f32[1024,512]{1,0:T(8,128)S(1)}, f32[1024,512]{1,0:T(8,128)}, u32[]{:S(2)}) copy-start(f32[1024,512]{1,0:T(8,128)} %param.5) | copy-start | bytes 6291460
  36.7 1.3 copy-start.1
  42.7 197.2 %all-gather.2.cloned.1.call-start = ((), (), s32[]{:S(2)}) async-start(), calls=%async_computation.1 | async-start | bytes 2621440 | tf_op jit(solution)/shard_map/all_gather | solution.py:34
  43.3 385.8 %all-reduce.5.cloned.1.call-start = ((), (), s32[]{:S(2)}) async-start(), calls=%async_computation.2 | async-start | bytes 2097152 | tf_op jit(solution)/shard_map/psum | solution.py:39
  429.0 3.8 copy-start.3
Sparse Core Ops, SparseCore 0:
  42.8 186.5 all-reduce.2
  246.1 182.8 all-reduce.4
Sparse Core Ops, SparseCore 1:
  45.1 37.0 all-gather.1
